TPU v7x, 512 devices: a whole 4x4x16 slice. The times are simulated.
512 devices in a mesh: blk: 128 (over x, z_lo, y), rep: 4 (over z_hi, core).
Axes of the slice: x: 4, y: 4, z: 16 (z_hi: 2, z_lo: 8; z = z_hi * 8 + z_lo), core: 2. Of those that a mesh axis runs over, the one named last changes fastest.
Arguments:
- queries: bfloat16 [16384, 512], P('blk'), may hold values from -3.59375 to 3.59375
- keys: bfloat16 [16384, 128], P('blk'), may hold values from -6 to 6
- values: bfloat16 [16384, 128], P('blk'), may hold values from -6 to 6
- output: bfloat16 [16384, 512], P('blk'), may hold values from -6 to 6
- grad_out: bfloat16 [16384, 512], P('blk'), may hold values from -6 to 6
- lse: float32 [4, 16384], P(None, 'blk'), may hold values from -1 to 12.5
- positions: int32 [16384], P('blk'), may hold values from 0 to 1073741823, as said below
Outputs:
- grad_queries: bfloat16 [16384, 512], P('blk')
- grad_keys: bfloat16 [16384, 128], P('blk')
- grad_values: bfloat16 [16384, 128], P('blk')
Inputs may be any that keep to these rules, and one draw needn't show every extreme that they name: positions are distinct. A token's place is the number of tokens with a smaller key. Cut the places into 2 n blocks of 64 consecutive places, n = 128; the rows of each index of blk hold the places of block c in order and then those of block 2 n - 1 - c in order, with c drawn at random for each index, every c once.
All inputs are finite; a program needn't handle non-finite values.
Results may differ from a plain program's by a relative error of at most 0.005.
Values may be sent and summed in bfloat16 or wider, within the bound.
A program may use at most 64 MiB of HBM per device.

v0:
```python
import jax
import jax.numpy as jnp
from jax import lax
from jax.sharding import PartitionSpec as P


def shifted_2(shard, axis, by):
    devices = lax.axis_size(axis)
    return lax.ppermute(shard, axis, [(i, (i + by) % devices) for i in range(devices)])


def pair_terms(
    score_scale,
    query_part,
    grad_part,
    lse_part,
    delta_part,
    query_pos,
    key_part,
    value_part,
    key_pos,
):
    scores = (
        jnp.einsum("pthd,pkd->phtk", query_part, key_part, preferred_element_type=jnp.float32)
        * score_scale
    )
    visible = key_pos[:, None, None, :] <= query_pos[:, None, :, None]
    probs = jnp.where(visible, jnp.exp(scores - lse_part[:, :, :, None]), 0.0)
    probs_low = probs.astype(jnp.bfloat16)
    value_terms = jnp.einsum(
        "phtk,pthd->pkd", probs_low, grad_part, preferred_element_type=jnp.float32
    )
    grad_probs = jnp.einsum(
        "pthd,pkd->phtk", grad_part, value_part, preferred_element_type=jnp.float32
    )
    grad_scores = (probs * (grad_probs - delta_part[:, :, :, None]) * score_scale).astype(
        jnp.bfloat16
    )
    query_terms = jnp.einsum(
        "phtk,pkd->pthd", grad_scores, key_part, preferred_element_type=jnp.float32
    )
    key_terms = jnp.einsum(
        "phtk,pthd->pkd", grad_scores, query_part, preferred_element_type=jnp.float32
    )
    pair_count = query_part.shape[0]
    part_rows = query_part.shape[1]
    return (query_terms.reshape(pair_count, part_rows, -1), key_terms, value_terms)


def moved(pair, amount):
    return shifted_2((pair[0], pair[1]), "blk", amount)


def carried(pair, amount):
    return shifted_2((pair[0], pair[1]), "blk", amount)


def pick(flags, first, second):
    shape = (flags.shape[0],) + (1,) * (first.ndim - 1)
    return jnp.where(flags.reshape(shape), first, second)


def per_device(queries, keys, values, output, grad_out, lse, positions):
    cycle_size = lax.axis_size("blk")
    group_size = lax.axis_size("rep")
    cycle_pos = lax.axis_index("blk")
    group = lax.axis_index("rep")
    tok_rows = keys.shape[0]
    half_rows = tok_rows // 2
    head_dim = keys.shape[1]
    head_count = queries.shape[1] // head_dim
    score_scale = head_dim ** (-0.5)
    quarter = cycle_size // group_size
    limit = 4
    window = min(limit, quarter)
    turn_count = quarter // window
    bit_count = group_size.bit_length() - 1
    query_heads = queries.reshape(tok_rows, head_count, head_dim)
    grad_heads = grad_out.reshape(tok_rows, head_count, head_dim)
    out_heads = output.reshape(tok_rows, head_count, head_dim)
    row_delta = jnp.sum(grad_heads.astype(jnp.float32) * out_heads.astype(jnp.float32), axis=2).T
    everyone = lax.all_gather(positions, "blk", axis=0, tiled=True).reshape(cycle_size, tok_rows)
    query_lo = query_heads[:half_rows]
    query_hi = query_heads[half_rows:]
    grad_lo = grad_heads[:half_rows]
    grad_hi = grad_heads[half_rows:]
    lse_lo = lse[:, :half_rows]
    lse_hi = lse[:, half_rows:]
    delta_lo = row_delta[:, :half_rows]
    delta_hi = row_delta[:, half_rows:]
    qpos_lo = positions[:half_rows]
    qpos_hi = positions[half_rows:]
    start_pair = (keys, values)
    for place in range(bit_count):
        shifted = moved(start_pair, quarter << place)
        chosen = group >> place & 1 == 1
        start_pair = (
            jnp.where(chosen, shifted[0], start_pair[0]),
            jnp.where(chosen, shifted[1], start_pair[1]),
        )
    win_keys = start_pair[0][None]
    win_values = start_pair[1][None]
    filled = 1
    while filled < window:
        step = min(filled, window - filled)
        extra = moved((win_keys, win_values), filled)
        win_keys = jnp.concatenate([win_keys, extra[0]], axis=0)
        win_values = jnp.concatenate([win_values, extra[1]], axis=0)
        filled = filled + step
    own_terms = pair_terms(
        score_scale,
        query_lo[None],
        grad_lo[None],
        lse_lo[None],
        delta_lo[None],
        qpos_lo[None],
        keys[:half_rows][None],
        values[:half_rows][None],
        qpos_lo[None],
    )
    own_weight = jnp.where(group == 0, 1.0, 0.0).astype(jnp.float32)
    grad_keys = jnp.zeros((window, tok_rows, head_dim), jnp.float32)
    grad_values = jnp.zeros((window, tok_rows, head_dim), jnp.float32)
    grad_query = jnp.zeros((tok_rows, head_count * head_dim), jnp.float32)
    members = jnp.arange(window, dtype=jnp.int32)

    def one_turn(turn, carry):
        win_keys, win_values, grad_keys, grad_values, grad_query = carry
        owners = (cycle_pos - quarter * group - members - window * turn) % cycle_size
        owner_pos = everyone[owners]
        lower = owner_pos[:, 0] < positions[0]
        key_lo = win_keys[:, :half_rows]
        key_hi = win_keys[:, half_rows:]
        value_lo = win_values[:, :half_rows]
        value_hi = win_values[:, half_rows:]
        kpos_lo = owner_pos[:, :half_rows]
        kpos_hi = owner_pos[:, half_rows:]
        pair_shape = (window * 2,)
        query_pair = jnp.stack(
            [
                jnp.broadcast_to(query_hi, (window,) + query_hi.shape),
                pick(
                    lower,
                    jnp.broadcast_to(query_lo, (window,) + query_lo.shape),
                    jnp.broadcast_to(query_hi, (window,) + query_hi.shape),
                ),
            ],
            axis=1,
        )
        grad_pair = jnp.stack(
            [
                jnp.broadcast_to(grad_hi, (window,) + grad_hi.shape),
                pick(
                    lower,
                    jnp.broadcast_to(grad_lo, (window,) + grad_lo.shape),
                    jnp.broadcast_to(grad_hi, (window,) + grad_hi.shape),
                ),
            ],
            axis=1,
        )
        lse_pair = jnp.stack(
            [
                jnp.broadcast_to(lse_hi, (window,) + lse_hi.shape),
                pick(
                    lower,
                    jnp.broadcast_to(lse_lo, (window,) + lse_lo.shape),
                    jnp.broadcast_to(lse_hi, (window,) + lse_hi.shape),
                ),
            ],
            axis=1,
        )
        delta_pair = jnp.stack(
            [
                jnp.broadcast_to(delta_hi, (window,) + delta_hi.shape),
                pick(
                    lower,
                    jnp.broadcast_to(delta_lo, (window,) + delta_lo.shape),
                    jnp.broadcast_to(delta_hi, (window,) + delta_hi.shape),
                ),
            ],
            axis=1,
        )
        qpos_pair = jnp.stack(
            [
                jnp.broadcast_to(qpos_hi, (window, half_rows)),
                pick(
                    lower,
                    jnp.broadcast_to(qpos_lo, (window, half_rows)),
                    jnp.broadcast_to(qpos_hi, (window, half_rows)),
                ),
            ],
            axis=1,
        )
        key_pair = jnp.stack([key_lo, pick(lower, key_lo, key_hi)], axis=1)
        value_pair = jnp.stack([value_lo, pick(lower, value_lo, value_hi)], axis=1)
        kpos_pair = jnp.stack([kpos_lo, pick(lower, kpos_lo, kpos_hi)], axis=1)
        terms = pair_terms(
            score_scale,
            query_pair.reshape(pair_shape + query_pair.shape[2:]),
            grad_pair.reshape(pair_shape + grad_pair.shape[2:]),
            lse_pair.reshape(pair_shape + lse_pair.shape[2:]),
            delta_pair.reshape(pair_shape + delta_pair.shape[2:]),
            qpos_pair.reshape(pair_shape + qpos_pair.shape[2:]),
            key_pair.reshape(pair_shape + key_pair.shape[2:]),
            value_pair.reshape(pair_shape + value_pair.shape[2:]),
            kpos_pair.reshape(pair_shape + kpos_pair.shape[2:]),
        )
        query_terms = terms[0].reshape(window, 2, half_rows, head_count * head_dim)
        key_terms = terms[1].reshape(window, 2, half_rows, head_dim)
        value_terms = terms[2].reshape(window, 2, half_rows, head_dim)
        zeros_query = jnp.zeros_like(query_terms[:, 1])
        add_lo = jnp.sum(pick(lower, query_terms[:, 1], zeros_query), axis=0)
        add_hi = jnp.sum(query_terms[:, 0], axis=0) + jnp.sum(
            pick(lower, zeros_query, query_terms[:, 1]), axis=0
        )
        grad_query = grad_query + jnp.concatenate([add_lo, add_hi], axis=0)
        zeros_key = jnp.zeros_like(key_terms[:, 1])
        key_add = jnp.concatenate(
            [
                key_terms[:, 0] + pick(lower, key_terms[:, 1], zeros_key),
                pick(lower, zeros_key, key_terms[:, 1]),
            ],
            axis=1,
        )
        value_add = jnp.concatenate(
            [
                value_terms[:, 0] + pick(lower, value_terms[:, 1], zeros_key),
                pick(lower, zeros_key, value_terms[:, 1]),
            ],
            axis=1,
        )
        grad_keys = grad_keys + key_add
        grad_values = grad_values + value_add
        win_keys, win_values = shifted_2((win_keys, win_values), "blk", window)
        grad_keys, grad_values = shifted_2((grad_keys, grad_values), "blk", window)
        return (win_keys, win_values, grad_keys, grad_values, grad_query)

    final = lax.fori_loop(
        0, turn_count, one_turn, (win_keys, win_values, grad_keys, grad_values, grad_query)
    )
    grad_keys = final[2]
    grad_values = final[3]
    grad_query = final[4]
    count = window
    while count > 1:
        lead = (count + 1) // 2
        extra = carried((grad_keys[lead:count], grad_values[lead:count]), -lead)
        tail = count - lead
        grad_keys = jnp.concatenate([grad_keys[:tail] + extra[0], grad_keys[tail:lead]], axis=0)
        grad_values = jnp.concatenate(
            [grad_values[:tail] + extra[1], grad_values[tail:lead]], axis=0
        )
        count = lead
    total_keys = grad_keys[0]
    total_values = grad_values[0]
    remaining = group_size - 1 - group
    for place in range(bit_count):
        shifted = carried((total_keys, total_values), quarter << place)
        chosen = remaining >> place & 1 == 1
        total_keys = jnp.where(chosen, shifted[0], total_keys)
        total_values = jnp.where(chosen, shifted[1], total_values)
    own_pad = jnp.zeros((half_rows, head_dim), jnp.float32)
    total_keys = total_keys + own_weight * jnp.concatenate([own_terms[1][0], own_pad], axis=0)
    total_values = total_values + own_weight * jnp.concatenate([own_terms[2][0], own_pad], axis=0)
    grad_query = grad_query + own_weight * jnp.concatenate(
        [own_terms[0][0], jnp.zeros((half_rows, head_count * head_dim), jnp.float32)], axis=0
    )
    summed = lax.psum((grad_query, total_keys, total_values), "rep")
    return (
        summed[0].astype(jnp.bfloat16),
        summed[1].astype(jnp.bfloat16),
        summed[2].astype(jnp.bfloat16),
    )


def solution(mesh):
    placed = (
        P("blk", None),
        P("blk", None),
        P("blk", None),
        P("blk", None),
        P("blk", None),
        P(None, "blk"),
        P("blk"),
    )
    return jax.shard_map(
        per_device,
        mesh=mesh,
        in_specs=placed,
        out_specs=(P("blk", None), P("blk", None), P("blk", None)),
        check_vma=False,
    )
```

profile of v0, /device:TPU:4, one launch (start us, length us, event | category | flops | bytes accessed | tf_op | source)
XLA Modules:
  0.0 912.1 jit_solution(14726433039888393091)
XLA Ops:
  0.6 3.1 collective-permute-start.4
  3.7 7.7 collective-permute-start.8
  18.9 481.2 %all-gather = s32[128,1,128]{2,1,0:T(1,128)S(1)} all-gather(s32[1,1,128]{2,1,0:T(1,128)S(1)} %bitcast.269), channel_id=1, replica_groups=mesh['blk'=128,'rep'=4] {'blk'}, dimensions={0}, use_global_device_ids=true | all-gather | bytes 66048 | tf_op jit(solution)/shard_map/all_gather | solution.py:82
  500.1 42.7 %collective-permute-start.5 = (bf16[128,128]{1,0:T(8,128)(2,1)S(1)}, bf16[128,128]{1,0:T(8,128)(2,1)S(1)}, u32[]{:S(2)}, u32[]{:S(2)}) collective-permute-start(bf16[128,128]{1,0:T(8,128)(2,1)S(1)} %broadcast_select_fusion.8), channel_id=1, source_target_pairs={{0,256},{4,260},{8,264},{12,268},{16,272},{20,276},{24,280},{28,28... | collective-permute-start | bytes 98312 | tf_op jit(solution)/shard_map/ppermute | solution.py:9
  547.0 3.2 collective-permute-done.9
  552.1 8.7 collective-permute-done.6
  562.7 2.9 collective-permute-done.10
  567.5 9.3 %collective-permute-done.7 = bf16[2,128,128]{2,1,0:T(8,128)(2,1)S(1)} collective-permute-done((bf16[2,128,128]{2,1,0:T(8,128)(2,1)S(1)}, bf16[2,128,128]{2,1,0:T(8,128)(2,1)S(1)}, u32[]{:S(2)}, u32[]{:S(2)}) %collective-permute-start.7) | collective-permute-done | bytes 65568 | tf_op jit(solution)/shard_map/ppermute | solution.py:9
  577.5 4.2 collective-permute-done.11
  582.4 238.4 %while.24 = (s32[]{:T(128)}, bf16[4,128,128]{2,1,0:T(8,128)(2,1)}, bf16[4,128,128]{2,1,0:T(8,128)(2,1)}, f32[4,128,128]{2,1,0:T(8,128)S(1)}, f32[4,128,128]{2,1,...) while((s32[]{:T(128)}, bf16[4,128,128]{2,1,0:T(8,128)(2,1)}, ...), condition=%wide.region_5.6_spmd.clone, body=%wide.region_1.5_spmd.clone.sunk | while | flops 171090496 | bytes 26398304 | solution.py:238
  598.3 3.8 collective-permute-done.1
  602.1 6.8 collective-permute-done.2
  628.3 3.4 collective-permute-done.1
  631.6 7.4 collective-permute-done.2
  658.4 3.3 collective-permute-done.1
  661.7 7.5 collective-permute-done.2
  688.5 3.3 collective-permute-done.1
  691.8 7.5 collective-permute-done.2
  718.6 3.3 collective-permute-done.1
  721.9 7.5 collective-permute-done.2
  752.0 7.6 collective-permute-done.2
  775.2 4.3 collective-permute-start.3
  781.4 7.1 collective-permute-done.2
  804.1 9.8 %collective-permute-start.3 = (f32[4,128,128]{2,1,0:T(8,128)}, f32[4,128,128]{2,1,0:T(8,128)S(1)}, u32[]{:S(2)}, u32[]{:S(2)}) collective-permute-start(f32[4,128,128]{2,1,0:T(8,128)} %maximum_add_fusion.7), channel_id=1, source_target_pairs={{0,16},{4,20},{8,24},{12,28},{16,32},{20,36},{24,40},{28,44},{32,4... | collective-permute-start | bytes 786440 | tf_op jit(solution)/shard_map/while/body/eval_jaxpr/ppermute | solution.py:9
  822.9 6.8 collective-permute-start.16
  832.3 9.9 %collective-permute-start.17 = (f32[1,128,128]{2,1,0:T(8,128)S(1)}, f32[1,128,128]{2,1,0:T(8,128)S(1)}, u32[]{:S(2)}, u32[]{:S(2)}) collective-permute-start(f32[1,128,128]{2,1,0:T(8,128)S(1)} %slice.266), channel_id=1, source_target_pairs={{0,508},{4,0},{8,4},{12,8},{16,12},{20,16},{24,20},{28,24},{32,28}... | collective-permute-start | bytes 196616 | tf_op jit(solution)/shard_map/ppermute | solution.py:9
  842.2 12.8 %collective-permute-start.14 = (f32[128,128]{1,0:T(8,128)S(1)}, f32[128,128]{1,0:T(8,128)S(1)}, u32[]{:S(2)}, u32[]{:S(2)}) collective-permute-start(f32[128,128]{1,0:T(8,128)S(1)} %fusion.30), channel_id=1, source_target_pairs={{0,128},{4,132},{8,136},{12,140},{16,144},{20,148},{24,152},{28,15... | collective-permute-start | bytes 196616 | tf_op jit(solution)/shard_map/ppermute | solution.py:9
  855.0 8.4 collective-permute-start.18
  863.5 4.2 collective-permute-start.15
  867.7 3.1 collective-permute-start.19
  871.1 4.3 collective-permute-done.19
  875.4 36.7 %all-reduce.5 = (bf16[128,512]{1,0:T(8,128)(2,1)}, bf16[128,128]{1,0:T(8,128)(2,1)}, bf16[128,128]{1,0:T(8,128)(2,1)}) all-reduce(f32[128,512]{1,0:T(8,128)S(1)} %multiply_add_fusion, f32[128,128]{1,0:T(8,128)S(1)} %multiply_add_fusion.2, f32[128,128]{1,0:T(8,128)S(1)} %multiply_add_fusion.1), channel_id=1, replica_groups=mesh['blk'=128,'rep'=4] {'rep'}, use_global_device_ids=true, to_apply=%region_6.7 | all-reduce | flops 98304 | bytes 589824 | tf_op jit(solution)/shard_map/psum | solution.py:268
  (657 shorter events, 176.6 us)
Async XLA Ops:
  0.6 499.5 %collective-permute-start.4 = (bf16[128,128]{1,0:T(8,128)(2,1)}, bf16[128,128]{1,0:T(8,128)(2,1)S(1)}, u32[]{:S(2)}, u32[]{:S(2)}) collective-permute-start(bf16[128,128]{1,0:T(8,128)(2,1)} %param.10), channel_id=1, source_target_pairs={{0,128},{4,132},{8,136},{12,140},{16,144},{20,148},{24,152},{28,15... | collective-permute-start | bytes 98312 | tf_op jit(solution)/shard_map/ppermute | solution.py:9
  3.7 539.1 %collective-permute-start.8 = (bf16[128,128]{1,0:T(8,128)(2,1)}, bf16[128,128]{1,0:T(8,128)(2,1)S(1)}, u32[]{:S(2)}, u32[]{:S(2)}) collective-permute-start(bf16[128,128]{1,0:T(8,128)(2,1)} %param.11), channel_id=1, source_target_pairs={{0,128},{4,132},{8,136},{12,140},{16,144},{20,148},{24,152},{28,15... | collective-permute-start | bytes 98312 | tf_op jit(solution)/shard_map/ppermute | solution.py:9
  500.1 44.9 %collective-permute-start.5 = (bf16[128,128]{1,0:T(8,128)(2,1)S(1)}, bf16[128,128]{1,0:T(8,128)(2,1)S(1)}, u32[]{:S(2)}, u32[]{:S(2)}) collective-permute-start(bf16[128,128]{1,0:T(8,128)(2,1)S(1)} %broadcast_select_fusion.8), channel_id=1, source_target_pairs={{0,256},{4,260},{8,264},{12,268},{16,272},{20,276},{24,280},{28,28... | collective-permute-start | bytes 98312 | tf_op jit(solution)/shard_map/ppermute | solution.py:9
  545.1 15.7 %collective-permute-start.6 = (bf16[1,128,128]{2,1,0:T(8,128)(2,1)S(1)}, bf16[1,128,128]{2,1,0:T(8,128)(2,1)S(1)}, u32[]{:S(2)}, u32[]{:S(2)}) collective-permute-start(bf16[1,128,128]{2,1,0:T(8,128)(2,1)S(1)} %select_bitcast_fusion.4), channel_id=1, source_target_pairs={{0,4},{4,8},{8,12},{12,16},{16,20},{20,24},{24,28},{28,32},{32,36}... | collective-permute-start | bytes 98312 | tf_op jit(solution)/shard_map/ppermute | solution.py:9
  550.2 15.4 %collective-permute-start.10 = (bf16[1,128,128]{2,1,0:T(8,128)(2,1)S(1)}, bf16[1,128,128]{2,1,0:T(8,128)(2,1)S(1)}, u32[]{:S(2)}, u32[]{:S(2)}) collective-permute-start(bf16[1,128,128]{2,1,0:T(8,128)(2,1)S(1)} %select_bitcast_fusion.3), channel_id=1, source_target_pairs={{0,4},{4,8},{8,12},{12,16},{16,20},{20,24},{24,28},{28,32},{32,36}... | collective-permute-start | bytes 98312 | tf_op jit(solution)/shard_map/ppermute | solution.py:9
  560.8 16.1 %collective-permute-start.7 = (bf16[2,128,128]{2,1,0:T(8,128)(2,1)S(1)}, bf16[2,128,128]{2,1,0:T(8,128)(2,1)S(1)}, u32[]{:S(2)}, u32[]{:S(2)}) collective-permute-start(bf16[2,128,128]{2,1,0:T(8,128)(2,1)S(1)} %pad_maximum_fusion.8), channel_id=1, source_target_pairs={{0,8},{4,12},{8,16},{12,20},{16,24},{20,28},{24,32},{28,36},{32,40... | collective-permute-start | bytes 196616 | tf_op jit(solution)/shard_map/ppermute | solution.py:9
  565.6 16.1 %collective-permute-start.11 = (bf16[2,128,128]{2,1,0:T(8,128)(2,1)S(1)}, bf16[2,128,128]{2,1,0:T(8,128)(2,1)S(1)}, u32[]{:S(2)}, u32[]{:S(2)}) collective-permute-start(bf16[2,128,128]{2,1,0:T(8,128)(2,1)S(1)} %pad_maximum_fusion.9), channel_id=1, source_target_pairs={{0,8},{4,12},{8,16},{12,20},{16,24},{20,28},{24,32},{28,36},{32,40... | collective-permute-start | bytes 196616 | tf_op jit(solution)/shard_map/ppermute | solution.py:9
  586.2 15.9 %collective-permute-start.1 = (bf16[4,128,128]{2,1,0:T(8,128)(2,1)S(1)}, bf16[4,128,128]{2,1,0:T(8,128)(2,1)}, u32[]{:S(2)}, u32[]{:S(2)}) collective-permute-start(bf16[4,128,128]{2,1,0:T(8,128)(2,1)S(1)} %copy.100), channel_id=1, source_target_pairs={{0,16},{4,20},{8,24},{12,28},{16,32},{20,36},{24,40},{28,44},{32,4... | collective-permute-start | bytes 393224 | tf_op jit(solution)/shard_map/while/body/eval_jaxpr/ppermute | solution.py:9
  591.9 17.1 %collective-permute-start.2 = (f32[4,128,128]{2,1,0:T(8,128)S(1)}, f32[4,128,128]{2,1,0:T(8,128)S(1)}, u32[]{:S(2)}, u32[]{:S(2)}) collective-permute-start(f32[4,128,128]{2,1,0:T(8,128)S(1)} %maximum_add_fusion.6), channel_id=1, source_target_pairs={{0,16},{4,20},{8,24},{12,28},{16,32},{20,36},{24,40},{28,44},{32,4... | collective-permute-start | bytes 786440 | tf_op jit(solution)/shard_map/while/body/eval_jaxpr/ppermute | solution.py:9
  594.5 17.2 %collective-permute-start.3 = (f32[4,128,128]{2,1,0:T(8,128)}, f32[4,128,128]{2,1,0:T(8,128)S(1)}, u32[]{:S(2)}, u32[]{:S(2)}) collective-permute-start(f32[4,128,128]{2,1,0:T(8,128)} %maximum_add_fusion.7), channel_id=1, source_target_pairs={{0,16},{4,20},{8,24},{12,28},{16,32},{20,36},{24,40},{28,44},{32,4... | collective-permute-start | bytes 786440 | tf_op jit(solution)/shard_map/while/body/eval_jaxpr/ppermute | solution.py:9
  616.2 15.4 %collective-permute-start.1 = (bf16[4,128,128]{2,1,0:T(8,128)(2,1)S(1)}, bf16[4,128,128]{2,1,0:T(8,128)(2,1)}, u32[]{:S(2)}, u32[]{:S(2)}) collective-permute-start(bf16[4,128,128]{2,1,0:T(8,128)(2,1)S(1)} %copy.100), channel_id=1, source_target_pairs={{0,16},{4,20},{8,24},{12,28},{16,32},{20,36},{24,40},{28,44},{32,4... | collective-permute-start | bytes 393224 | tf_op jit(solution)/shard_map/while/body/eval_jaxpr/ppermute | solution.py:9
  621.9 17.1 %collective-permute-start.2 = (f32[4,128,128]{2,1,0:T(8,128)S(1)}, f32[4,128,128]{2,1,0:T(8,128)S(1)}, u32[]{:S(2)}, u32[]{:S(2)}) collective-permute-start(f32[4,128,128]{2,1,0:T(8,128)S(1)} %maximum_add_fusion.6), channel_id=1, source_target_pairs={{0,16},{4,20},{8,24},{12,28},{16,32},{20,36},{24,40},{28,44},{32,4... | collective-permute-start | bytes 786440 | tf_op jit(solution)/shard_map/while/body/eval_jaxpr/ppermute | solution.py:9
  624.5 17.3 %collective-permute-start.3 = (f32[4,128,128]{2,1,0:T(8,128)}, f32[4,128,128]{2,1,0:T(8,128)S(1)}, u32[]{:S(2)}, u32[]{:S(2)}) collective-permute-start(f32[4,128,128]{2,1,0:T(8,128)} %maximum_add_fusion.7), channel_id=1, source_target_pairs={{0,16},{4,20},{8,24},{12,28},{16,32},{20,36},{24,40},{28,44},{32,4... | collective-permute-start | bytes 786440 | tf_op jit(solution)/shard_map/while/body/eval_jaxpr/ppermute | solution.py:9
  646.3 15.3 %collective-permute-start.1 = (bf16[4,128,128]{2,1,0:T(8,128)(2,1)S(1)}, bf16[4,128,128]{2,1,0:T(8,128)(2,1)}, u32[]{:S(2)}, u32[]{:S(2)}) collective-permute-start(bf16[4,128,128]{2,1,0:T(8,128)(2,1)S(1)} %copy.100), channel_id=1, source_target_pairs={{0,16},{4,20},{8,24},{12,28},{16,32},{20,36},{24,40},{28,44},{32,4... | collective-permute-start | bytes 393224 | tf_op jit(solution)/shard_map/while/body/eval_jaxpr/ppermute | solution.py:9
  652.0 17.1 %collective-permute-start.2 = (f32[4,128,128]{2,1,0:T(8,128)S(1)}, f32[4,128,128]{2,1,0:T(8,128)S(1)}, u32[]{:S(2)}, u32[]{:S(2)}) collective-permute-start(f32[4,128,128]{2,1,0:T(8,128)S(1)} %maximum_add_fusion.6), channel_id=1, source_target_pairs={{0,16},{4,20},{8,24},{12,28},{16,32},{20,36},{24,40},{28,44},{32,4... | collective-permute-start | bytes 786440 | tf_op jit(solution)/shard_map/while/body/eval_jaxpr/ppermute | solution.py:9
  654.7 17.3 %collective-permute-start.3 = (f32[4,128,128]{2,1,0:T(8,128)}, f32[4,128,128]{2,1,0:T(8,128)S(1)}, u32[]{:S(2)}, u32[]{:S(2)}) collective-permute-start(f32[4,128,128]{2,1,0:T(8,128)} %maximum_add_fusion.7), channel_id=1, source_target_pairs={{0,16},{4,20},{8,24},{12,28},{16,32},{20,36},{24,40},{28,44},{32,4... | collective-permute-start | bytes 786440 | tf_op jit(solution)/shard_map/while/body/eval_jaxpr/ppermute | solution.py:9
  682.1 17.1 %collective-permute-start.2 = (f32[4,128,128]{2,1,0:T(8,128)S(1)}, f32[4,128,128]{2,1,0:T(8,128)S(1)}, u32[]{:S(2)}, u32[]{:S(2)}) collective-permute-start(f32[4,128,128]{2,1,0:T(8,128)S(1)} %maximum_add_fusion.6), channel_id=1, source_target_pairs={{0,16},{4,20},{8,24},{12,28},{16,32},{20,36},{24,40},{28,44},{32,4... | collective-permute-start | bytes 786440 | tf_op jit(solution)/shard_map/while/body/eval_jaxpr/ppermute | solution.py:9
  684.8 17.3 %collective-permute-start.3 = (f32[4,128,128]{2,1,0:T(8,128)}, f32[4,128,128]{2,1,0:T(8,128)S(1)}, u32[]{:S(2)}, u32[]{:S(2)}) collective-permute-start(f32[4,128,128]{2,1,0:T(8,128)} %maximum_add_fusion.7), channel_id=1, source_target_pairs={{0,16},{4,20},{8,24},{12,28},{16,32},{20,36},{24,40},{28,44},{32,4... | collective-permute-start | bytes 786440 | tf_op jit(solution)/shard_map/while/body/eval_jaxpr/ppermute | solution.py:9
  712.2 17.1 %collective-permute-start.2 = (f32[4,128,128]{2,1,0:T(8,128)S(1)}, f32[4,128,128]{2,1,0:T(8,128)S(1)}, u32[]{:S(2)}, u32[]{:S(2)}) collective-permute-start(f32[4,128,128]{2,1,0:T(8,128)S(1)} %maximum_add_fusion.6), channel_id=1, source_target_pairs={{0,16},{4,20},{8,24},{12,28},{16,32},{20,36},{24,40},{28,44},{32,4... | collective-permute-start | bytes 786440 | tf_op jit(solution)/shard_map/while/body/eval_jaxpr/ppermute | solution.py:9
  714.9 17.3 %collective-permute-start.3 = (f32[4,128,128]{2,1,0:T(8,128)}, f32[4,128,128]{2,1,0:T(8,128)S(1)}, u32[]{:S(2)}, u32[]{:S(2)}) collective-permute-start(f32[4,128,128]{2,1,0:T(8,128)} %maximum_add_fusion.7), channel_id=1, source_target_pairs={{0,16},{4,20},{8,24},{12,28},{16,32},{20,36},{24,40},{28,44},{32,4... | collective-permute-start | bytes 786440 | tf_op jit(solution)/shard_map/while/body/eval_jaxpr/ppermute | solution.py:9
  733.8 15.8 %collective-permute-start = (bf16[4,128,128]{2,1,0:T(8,128)(2,1)S(1)}, bf16[4,128,128]{2,1,0:T(8,128)(2,1)}, u32[]{:S(2)}, u32[]{:S(2)}) collective-permute-start(bf16[4,128,128]{2,1,0:T(8,128)(2,1)S(1)} %copy.99), channel_id=1, source_target_pairs={{0,16},{4,20},{8,24},{12,28},{16,32},{20,36},{24,40},{28,44},{32,4... | collective-permute-start | bytes 393224 | tf_op jit(solution)/shard_map/while/body/eval_jaxpr/ppermute | solution.py:9
  742.3 17.3 %collective-permute-start.2 = (f32[4,128,128]{2,1,0:T(8,128)S(1)}, f32[4,128,128]{2,1,0:T(8,128)S(1)}, u32[]{:S(2)}, u32[]{:S(2)}) collective-permute-start(f32[4,128,128]{2,1,0:T(8,128)S(1)} %maximum_add_fusion.6), channel_id=1, source_target_pairs={{0,16},{4,20},{8,24},{12,28},{16,32},{20,36},{24,40},{28,44},{32,4... | collective-permute-start | bytes 786440 | tf_op jit(solution)/shard_map/while/body/eval_jaxpr/ppermute | solution.py:9
  745.0 17.4 %collective-permute-start.3 = (f32[4,128,128]{2,1,0:T(8,128)}, f32[4,128,128]{2,1,0:T(8,128)S(1)}, u32[]{:S(2)}, u32[]{:S(2)}) collective-permute-start(f32[4,128,128]{2,1,0:T(8,128)} %maximum_add_fusion.7), channel_id=1, source_target_pairs={{0,16},{4,20},{8,24},{12,28},{16,32},{20,36},{24,40},{28,44},{32,4... | collective-permute-start | bytes 786440 | tf_op jit(solution)/shard_map/while/body/eval_jaxpr/ppermute | solution.py:9
  764.1 17.2 %collective-permute-start = (bf16[4,128,128]{2,1,0:T(8,128)(2,1)S(1)}, bf16[4,128,128]{2,1,0:T(8,128)(2,1)}, u32[]{:S(2)}, u32[]{:S(2)}) collective-permute-start(bf16[4,128,128]{2,1,0:T(8,128)(2,1)S(1)} %copy.99), channel_id=1, source_target_pairs={{0,16},{4,20},{8,24},{12,28},{16,32},{20,36},{24,40},{28,44},{32,4... | collective-permute-start | bytes 393224 | tf_op jit(solution)/shard_map/while/body/eval_jaxpr/ppermute | solution.py:9
  772.6 15.9 %collective-permute-start.2 = (f32[4,128,128]{2,1,0:T(8,128)S(1)}, f32[4,128,128]{2,1,0:T(8,128)S(1)}, u32[]{:S(2)}, u32[]{:S(2)}) collective-permute-start(f32[4,128,128]{2,1,0:T(8,128)S(1)} %maximum_add_fusion.6), channel_id=1, source_target_pairs={{0,16},{4,20},{8,24},{12,28},{16,32},{20,36},{24,40},{28,44},{32,4... | collective-permute-start | bytes 786440 | tf_op jit(solution)/shard_map/while/body/eval_jaxpr/ppermute | solution.py:9
  775.2 16.0 %collective-permute-start.3 = (f32[4,128,128]{2,1,0:T(8,128)}, f32[4,128,128]{2,1,0:T(8,128)S(1)}, u32[]{:S(2)}, u32[]{:S(2)}) collective-permute-start(f32[4,128,128]{2,1,0:T(8,128)} %maximum_add_fusion.7), channel_id=1, source_target_pairs={{0,16},{4,20},{8,24},{12,28},{16,32},{20,36},{24,40},{28,44},{32,4... | collective-permute-start | bytes 786440 | tf_op jit(solution)/shard_map/while/body/eval_jaxpr/ppermute | solution.py:9
  792.9 22.7 %collective-permute-start = (bf16[4,128,128]{2,1,0:T(8,128)(2,1)S(1)}, bf16[4,128,128]{2,1,0:T(8,128)(2,1)}, u32[]{:S(2)}, u32[]{:S(2)}) collective-permute-start(bf16[4,128,128]{2,1,0:T(8,128)(2,1)S(1)} %copy.99), channel_id=1, source_target_pairs={{0,16},{4,20},{8,24},{12,28},{16,32},{20,36},{24,40},{28,44},{32,4... | collective-permute-start | bytes 393224 | tf_op jit(solution)/shard_map/while/body/eval_jaxpr/ppermute | solution.py:9
  795.7 19.9 %collective-permute-start.1 = (bf16[4,128,128]{2,1,0:T(8,128)(2,1)S(1)}, bf16[4,128,128]{2,1,0:T(8,128)(2,1)}, u32[]{:S(2)}, u32[]{:S(2)}) collective-permute-start(bf16[4,128,128]{2,1,0:T(8,128)(2,1)S(1)} %copy.100), channel_id=1, source_target_pairs={{0,16},{4,20},{8,24},{12,28},{16,32},{20,36},{24,40},{28,44},{32,4... | collective-permute-start | bytes 393224 | tf_op jit(solution)/shard_map/while/body/eval_jaxpr/ppermute | solution.py:9
  801.4 15.8 %collective-permute-start.2 = (f32[4,128,128]{2,1,0:T(8,128)S(1)}, f32[4,128,128]{2,1,0:T(8,128)S(1)}, u32[]{:S(2)}, u32[]{:S(2)}) collective-permute-start(f32[4,128,128]{2,1,0:T(8,128)S(1)} %maximum_add_fusion.6), channel_id=1, source_target_pairs={{0,16},{4,20},{8,24},{12,28},{16,32},{20,36},{24,40},{28,44},{32,4... | collective-permute-start | bytes 786440 | tf_op jit(solution)/shard_map/while/body/eval_jaxpr/ppermute | solution.py:9
  804.1 16.0 %collective-permute-start.3 = (f32[4,128,128]{2,1,0:T(8,128)}, f32[4,128,128]{2,1,0:T(8,128)S(1)}, u32[]{:S(2)}, u32[]{:S(2)}) collective-permute-start(f32[4,128,128]{2,1,0:T(8,128)} %maximum_add_fusion.7), channel_id=1, source_target_pairs={{0,16},{4,20},{8,24},{12,28},{16,32},{20,36},{24,40},{28,44},{32,4... | collective-permute-start | bytes 786440 | tf_op jit(solution)/shard_map/while/body/eval_jaxpr/ppermute | solution.py:9
  832.3 22.7 %collective-permute-start.17 = (f32[1,128,128]{2,1,0:T(8,128)S(1)}, f32[1,128,128]{2,1,0:T(8,128)S(1)}, u32[]{:S(2)}, u32[]{:S(2)}) collective-permute-start(f32[1,128,128]{2,1,0:T(8,128)S(1)} %slice.266), channel_id=1, source_target_pairs={{0,508},{4,0},{8,4},{12,8},{16,12},{20,16},{24,20},{28,24},{32,28}... | collective-permute-start | bytes 196616 | tf_op jit(solution)/shard_map/ppermute | solution.py:9
  842.2 21.2 %collective-permute-start.14 = (f32[128,128]{1,0:T(8,128)S(1)}, f32[128,128]{1,0:T(8,128)S(1)}, u32[]{:S(2)}, u32[]{:S(2)}) collective-permute-start(f32[128,128]{1,0:T(8,128)S(1)} %fusion.30), channel_id=1, source_target_pairs={{0,128},{4,132},{8,136},{12,140},{16,144},{20,148},{24,152},{28,15... | collective-permute-start | bytes 196616 | tf_op jit(solution)/shard_map/ppermute | solution.py:9
  (129 other events, 858.1 us)
where the time goes:
time: 914 us; the launch traced here: 912 us
  blocking collectives  518 us (57%)
  starting transfers between devices  185 us (20%)
  waiting for transfers between devices  128 us (14%)
  local copies, waits for them, and re-layouts  39.5 us (4%)
  matrix products  19.5 us (2%)
  other arithmetic  18.2 us (2%)
    all_gather x1, blocking collectives, per_device(): lax.all_gather(positions, 'blk', axis=0, tiled=True)  481 us
    ppermute x48, starting transfers between devices, shifted_2(): lax.ppermute(shard, axis, [(i, (i + by) % devices) for i in range(devices)])  185 us
    ppermute x48, waiting for transfers between devices, shifted_2(): lax.ppermute(shard, axis, [(i, (i + by) % devices) for i in range(devices)])  128 us
    psum x1, blocking collectives, per_device(): summed = lax.psum((grad_query, total_keys, total_values), 'rep')  36.7 us
    while x224, local copies, waits for them, and re-layouts  20.4 us
  transfers between devices with their start and end apart: 48, of which 31 were waited for; matrix products, arithmetic and copies ran while one was open for 7% of the time, Pallas kernels for 0%

commit v1 on v0

--- a/solution.py
+++ b/solution.py
@@ -2,6 +2,11 @@
 import jax.numpy as jnp
 from jax import lax
 from jax.sharding import PartitionSpec as P
+
+
+def exchange_gather(x, mesh_axis, dim):
+    sent = jnp.stack([x] * lax.axis_size(mesh_axis))
+    return jnp.concatenate(lax.all_to_all(sent, mesh_axis, 0, 0), axis=dim)
 
 
 def shifted_2(shard, axis, by):
@@ -79,7 +84,7 @@
     grad_heads = grad_out.reshape(tok_rows, head_count, head_dim)
     out_heads = output.reshape(tok_rows, head_count, head_dim)
     row_delta = jnp.sum(grad_heads.astype(jnp.float32) * out_heads.astype(jnp.float32), axis=2).T
-    everyone = lax.all_gather(positions, "blk", axis=0, tiled=True).reshape(cycle_size, tok_rows)
+    everyone = exchange_gather(positions, "blk", 0).reshape(cycle_size, tok_rows)
     query_lo = query_heads[:half_rows]
     query_hi = query_heads[half_rows:]
     grad_lo = grad_heads[:half_rows]

time: 914 us -> 412 us (0.45)
  the two profiles are of different devices: /device:TPU:4 before, /device:TPU:8 now
where the time goes in v1:
time: 412 us; the launch traced here: 410 us
  starting transfers between devices  145 us (35%)
  waiting for transfers between devices  140 us (34%)
  blocking collectives  43.2 us (10%)
  local copies, waits for them, and re-layouts  39.5 us (10%)
  matrix products  19.5 us (5%)
  other arithmetic  18.1 us (4%)
    ppermute x48, waiting for transfers between devices, shifted_2(): lax.ppermute(shard, axis, [(i, (i + by) % devices) for i in range(devices)])  140 us
    ppermute x48, starting transfers between devices, shifted_2(): lax.ppermute(shard, axis, [(i, (i + by) % devices) for i in range(devices)])  127 us
    psum x1, blocking collectives, per_device(): summed = lax.psum((grad_query, total_keys, total_values), 'rep')  43.2 us
    while x224, local copies, waits for them, and re-layouts  20.2 us
    all_to_all x1, starting transfers between devices, exchange_gather(): return jnp.concatenate(lax.all_to_all(sent, mesh_axis, 0, 0), axis=dim)  18.3 us
  transfers between devices with their start and end apart: 49, of which 40 were waited for; matrix products, arithmetic and copies ran while one was open for 15% of the time, Pallas kernels for 0%

profile of v1, /device:TPU:8, one launch (start us, length us, event | category | flops | bytes accessed | tf_op | source)
XLA Modules:
  0.0 409.9 jit_solution(14919865831735459916)
XLA Ops:
  0.6 3.5 collective-permute-start.4
  4.2 3.4 collective-permute-start.8
  8.9 18.3 %all-to-all-start = ((s32[128,1,128]{2,1,0:T(1,128)}), s32[128,1,128]{2,1,0:T(1,128)S(1)}, u32[]{:S(2)}, u32[]{:S(2)}) async-start(s32[128,1,128]{2,1,0:T(1,128)} %stack.138), calls=%async_computation | async-start | bytes 131072 | tf_op jit(solution)/shard_map/all_to_all | solution.py:9
  33.5 5.2 %collective-permute-start.5 = (bf16[128,128]{1,0:T(8,128)(2,1)S(1)}, bf16[128,128]{1,0:T(8,128)(2,1)S(1)}, u32[]{:S(2)}, u32[]{:S(2)}) collective-permute-start(bf16[128,128]{1,0:T(8,128)(2,1)S(1)} %broadcast_select_fusion.8), channel_id=1, source_target_pairs={{0,256},{4,260},{8,264},{12,268},{16,272},{20,276},{24,280},{28,28... | collective-permute-start | bytes 98312 | tf_op jit(solution)/shard_map/ppermute | solution.py:14
  40.9 3.4 collective-permute-start.6
  46.1 3.4 collective-permute-start.10
  49.5 4.0 collective-permute-start.7
  53.5 4.3 %collective-permute-start.11 = (bf16[2,128,128]{2,1,0:T(8,128)(2,1)S(1)}, bf16[2,128,128]{2,1,0:T(8,128)(2,1)S(1)}, u32[]{:S(2)}, u32[]{:S(2)}) collective-permute-start(bf16[2,128,128]{2,1,0:T(8,128)(2,1)S(1)} %pad_maximum_fusion.9), channel_id=1, source_target_pairs={{0,8},{4,12},{8,16},{12,20},{16,24},{20,28},{24,32},{28,36},{32,40... | collective-permute-start | bytes 196616 | tf_op jit(solution)/shard_map/ppermute | solution.py:14
  57.8 9.4 %collective-permute-done.7 = bf16[2,128,128]{2,1,0:T(8,128)(2,1)S(1)} collective-permute-done((bf16[2,128,128]{2,1,0:T(8,128)(2,1)S(1)}, bf16[2,128,128]{2,1,0:T(8,128)(2,1)S(1)}, u32[]{:S(2)}, u32[]{:S(2)}) %collective-permute-start.7) | collective-permute-done | bytes 65568 | tf_op jit(solution)/shard_map/ppermute | solution.py:14
  71.5 250.6 %while.24 = (s32[]{:T(128)}, bf16[4,128,128]{2,1,0:T(8,128)(2,1)}, bf16[4,128,128]{2,1,0:T(8,128)(2,1)}, f32[4,128,128]{2,1,0:T(8,128)S(1)}, f32[4,128,128]{2,1,...) while((s32[]{:T(128)}, bf16[4,128,128]{2,1,0:T(8,128)(2,1)}, ...), condition=%wide.region_5.6_spmd.clone, body=%wide.region_1.5_spmd.clone.sunk | while | flops 171090496 | bytes 26398304 | solution.py:243
  88.2 3.2 collective-permute-done.1
  91.4 7.9 %collective-permute-done.2 = f32[4,128,128]{2,1,0:T(8,128)S(1)} collective-permute-done((f32[4,128,128]{2,1,0:T(8,128)S(1)}, f32[4,128,128]{2,1,0:T(8,128)S(1)}, u32[]{:S(2)}, u32[]{:S(2)}) %collective-permute-start.2) | collective-permute-done | bytes 262176 | tf_op jit(solution)/shard_map/while/body/eval_jaxpr/ppermute | solution.py:14
  119.5 3.7 collective-permute-done.1
  123.1 7.5 %collective-permute-done.2 = f32[4,128,128]{2,1,0:T(8,128)S(1)} collective-permute-done((f32[4,128,128]{2,1,0:T(8,128)S(1)}, f32[4,128,128]{2,1,0:T(8,128)S(1)}, u32[]{:S(2)}, u32[]{:S(2)}) %collective-permute-start.2) | collective-permute-done | bytes 262176 | tf_op jit(solution)/shard_map/while/body/eval_jaxpr/ppermute | solution.py:14
  150.8 3.7 collective-permute-done.1
  154.4 7.5 %collective-permute-done.2 = f32[4,128,128]{2,1,0:T(8,128)S(1)} collective-permute-done((f32[4,128,128]{2,1,0:T(8,128)S(1)}, f32[4,128,128]{2,1,0:T(8,128)S(1)}, u32[]{:S(2)}, u32[]{:S(2)}) %collective-permute-start.2) | collective-permute-done | bytes 262176 | tf_op jit(solution)/shard_map/while/body/eval_jaxpr/ppermute | solution.py:14
  182.1 3.7 collective-permute-done.1
  185.7 7.5 %collective-permute-done.2 = f32[4,128,128]{2,1,0:T(8,128)S(1)} collective-permute-done((f32[4,128,128]{2,1,0:T(8,128)S(1)}, f32[4,128,128]{2,1,0:T(8,128)S(1)}, u32[]{:S(2)}, u32[]{:S(2)}) %collective-permute-start.2) | collective-permute-done | bytes 262176 | tf_op jit(solution)/shard_map/while/body/eval_jaxpr/ppermute | solution.py:14
  213.4 3.7 collective-permute-done.1
  217.0 7.5 %collective-permute-done.2 = f32[4,128,128]{2,1,0:T(8,128)S(1)} collective-permute-done((f32[4,128,128]{2,1,0:T(8,128)S(1)}, f32[4,128,128]{2,1,0:T(8,128)S(1)}, u32[]{:S(2)}, u32[]{:S(2)}) %collective-permute-start.2) | collective-permute-done | bytes 262176 | tf_op jit(solution)/shard_map/while/body/eval_jaxpr/ppermute | solution.py:14
  244.7 3.7 collective-permute-done.1
  248.3 7.5 %collective-permute-done.2 = f32[4,128,128]{2,1,0:T(8,128)S(1)} collective-permute-done((f32[4,128,128]{2,1,0:T(8,128)S(1)}, f32[4,128,128]{2,1,0:T(8,128)S(1)}, u32[]{:S(2)}, u32[]{:S(2)}) %collective-permute-start.2) | collective-permute-done | bytes 262176 | tf_op jit(solution)/shard_map/while/body/eval_jaxpr/ppermute | solution.py:14
  276.0 3.7 collective-permute-done.1
  279.6 7.5 %collective-permute-done.2 = f32[4,128,128]{2,1,0:T(8,128)S(1)} collective-permute-done((f32[4,128,128]{2,1,0:T(8,128)S(1)}, f32[4,128,128]{2,1,0:T(8,128)S(1)}, u32[]{:S(2)}, u32[]{:S(2)}) %collective-permute-start.2) | collective-permute-done | bytes 262176 | tf_op jit(solution)/shard_map/while/body/eval_jaxpr/ppermute | solution.py:14
  307.3 3.8 collective-permute-done.1
  311.0 7.5 %collective-permute-done.2 = f32[4,128,128]{2,1,0:T(8,128)S(1)} collective-permute-done((f32[4,128,128]{2,1,0:T(8,128)S(1)}, f32[4,128,128]{2,1,0:T(8,128)S(1)}, u32[]{:S(2)}, u32[]{:S(2)}) %collective-permute-start.2) | collective-permute-done | bytes 262176 | tf_op jit(solution)/shard_map/while/body/eval_jaxpr/ppermute | solution.py:14
  324.2 9.5 %collective-permute-start.16 = (f32[2,128,128]{2,1,0:T(8,128)S(1)}, f32[2,128,128]{2,1,0:T(8,128)S(1)}, u32[]{:S(2)}, u32[]{:S(2)}) collective-permute-start(f32[2,128,128]{2,1,0:T(8,128)S(1)} %slice.236), channel_id=1, source_target_pairs={{0,504},{4,508},{8,0},{12,4},{16,8},{20,12},{24,16},{28,20},{32,24... | collective-permute-start | bytes 393224 | tf_op jit(solution)/shard_map/ppermute | solution.py:14
  333.8 11.7 %collective-permute-start.13 = (f32[1,128,128]{2,1,0:T(8,128)S(1)}, f32[1,128,128]{2,1,0:T(8,128)S(1)}, u32[]{:S(2)}, u32[]{:S(2)}) collective-permute-start(f32[1,128,128]{2,1,0:T(8,128)S(1)} %slice.264), channel_id=1, source_target_pairs={{0,508},{4,0},{8,4},{12,8},{16,12},{20,16},{24,20},{28,24},{32,28}... | collective-permute-start | bytes 196616 | tf_op jit(solution)/shard_map/ppermute | solution.py:14
  355.4 3.1 collective-permute-start.15
  359.1 3.7 collective-permute-start.19
  363.1 3.7 collective-permute-done.19
  366.8 43.2 %all-reduce.5 = (bf16[128,512]{1,0:T(8,128)(2,1)}, bf16[128,128]{1,0:T(8,128)(2,1)}, bf16[128,128]{1,0:T(8,128)(2,1)}) all-reduce(f32[128,512]{1,0:T(8,128)S(1)} %multiply_add_fusion, f32[128,128]{1,0:T(8,128)S(1)} %multiply_add_fusion.2, f32[128,128]{1,0:T(8,128)S(1)} %multiply_add_fusion.1), channel_id=1, replica_groups=mesh['blk'=128,'rep'=4] {'rep'}, use_global_device_ids=true, to_apply=%region_6.7 | all-reduce | flops 98304 | bytes 589824 | tf_op jit(solution)/shard_map/psum | solution.py:273
  (661 shorter events, 186.8 us)
Async XLA Ops:
  0.6 32.8 %collective-permute-start.4 = (bf16[128,128]{1,0:T(8,128)(2,1)}, bf16[128,128]{1,0:T(8,128)(2,1)S(1)}, u32[]{:S(2)}, u32[]{:S(2)}) collective-permute-start(bf16[128,128]{1,0:T(8,128)(2,1)} %param.10), channel_id=1, source_target_pairs={{0,128},{4,132},{8,136},{12,140},{16,144},{20,148},{24,152},{28,15... | collective-permute-start | bytes 98312 | tf_op jit(solution)/shard_map/ppermute | solution.py:14
  4.2 34.5 %collective-permute-start.8 = (bf16[128,128]{1,0:T(8,128)(2,1)}, bf16[128,128]{1,0:T(8,128)(2,1)S(1)}, u32[]{:S(2)}, u32[]{:S(2)}) collective-permute-start(bf16[128,128]{1,0:T(8,128)(2,1)} %param.11), channel_id=1, source_target_pairs={{0,128},{4,132},{8,136},{12,140},{16,144},{20,148},{24,152},{28,15... | collective-permute-start | bytes 98312 | tf_op jit(solution)/shard_map/ppermute | solution.py:14
  8.9 62.5 %all-to-all-start = ((s32[128,1,128]{2,1,0:T(1,128)}), s32[128,1,128]{2,1,0:T(1,128)S(1)}, u32[]{:S(2)}, u32[]{:S(2)}) async-start(s32[128,1,128]{2,1,0:T(1,128)} %stack.138), calls=%async_computation | async-start | bytes 131072 | tf_op jit(solution)/shard_map/all_to_all | solution.py:9
  49.5 17.8 %collective-permute-start.7 = (bf16[2,128,128]{2,1,0:T(8,128)(2,1)S(1)}, bf16[2,128,128]{2,1,0:T(8,128)(2,1)S(1)}, u32[]{:S(2)}, u32[]{:S(2)}) collective-permute-start(bf16[2,128,128]{2,1,0:T(8,128)(2,1)S(1)} %pad_maximum_fusion.8), channel_id=1, source_target_pairs={{0,8},{4,12},{8,16},{12,20},{16,24},{20,28},{24,32},{28,36},{32,40... | collective-permute-start | bytes 196616 | tf_op jit(solution)/shard_map/ppermute | solution.py:14
  53.5 17.3 %collective-permute-start.11 = (bf16[2,128,128]{2,1,0:T(8,128)(2,1)S(1)}, bf16[2,128,128]{2,1,0:T(8,128)(2,1)S(1)}, u32[]{:S(2)}, u32[]{:S(2)}) collective-permute-start(bf16[2,128,128]{2,1,0:T(8,128)(2,1)S(1)} %pad_maximum_fusion.9), channel_id=1, source_target_pairs={{0,8},{4,12},{8,16},{12,20},{16,24},{20,28},{24,32},{28,36},{32,40... | collective-permute-start | bytes 196616 | tf_op jit(solution)/shard_map/ppermute | solution.py:14
  75.3 16.0 %collective-permute-start.1 = (bf16[4,128,128]{2,1,0:T(8,128)(2,1)S(1)}, bf16[4,128,128]{2,1,0:T(8,128)(2,1)}, u32[]{:S(2)}, u32[]{:S(2)}) collective-permute-start(bf16[4,128,128]{2,1,0:T(8,128)(2,1)S(1)} %copy.100), channel_id=1, source_target_pairs={{0,16},{4,20},{8,24},{12,28},{16,32},{20,36},{24,40},{28,44},{32,4... | collective-permute-start | bytes 393224 | tf_op jit(solution)/shard_map/while/body/eval_jaxpr/ppermute | solution.py:14
  81.0 18.3 %collective-permute-start.2 = (f32[4,128,128]{2,1,0:T(8,128)S(1)}, f32[4,128,128]{2,1,0:T(8,128)S(1)}, u32[]{:S(2)}, u32[]{:S(2)}) collective-permute-start(f32[4,128,128]{2,1,0:T(8,128)S(1)} %maximum_add_fusion.6), channel_id=1, source_target_pairs={{0,16},{4,20},{8,24},{12,28},{16,32},{20,36},{24,40},{28,44},{32,4... | collective-permute-start | bytes 786440 | tf_op jit(solution)/shard_map/while/body/eval_jaxpr/ppermute | solution.py:14
  83.6 18.5 %collective-permute-start.3 = (f32[4,128,128]{2,1,0:T(8,128)}, f32[4,128,128]{2,1,0:T(8,128)S(1)}, u32[]{:S(2)}, u32[]{:S(2)}) collective-permute-start(f32[4,128,128]{2,1,0:T(8,128)} %maximum_add_fusion.7), channel_id=1, source_target_pairs={{0,16},{4,20},{8,24},{12,28},{16,32},{20,36},{24,40},{28,44},{32,4... | collective-permute-start | bytes 786440 | tf_op jit(solution)/shard_map/while/body/eval_jaxpr/ppermute | solution.py:14
  103.8 15.7 %collective-permute-start = (bf16[4,128,128]{2,1,0:T(8,128)(2,1)S(1)}, bf16[4,128,128]{2,1,0:T(8,128)(2,1)}, u32[]{:S(2)}, u32[]{:S(2)}) collective-permute-start(bf16[4,128,128]{2,1,0:T(8,128)(2,1)S(1)} %copy.99), channel_id=1, source_target_pairs={{0,16},{4,20},{8,24},{12,28},{16,32},{20,36},{24,40},{28,44},{32,4... | collective-permute-start | bytes 393224 | tf_op jit(solution)/shard_map/while/body/eval_jaxpr/ppermute | solution.py:14
  106.6 16.5 %collective-permute-start.1 = (bf16[4,128,128]{2,1,0:T(8,128)(2,1)S(1)}, bf16[4,128,128]{2,1,0:T(8,128)(2,1)}, u32[]{:S(2)}, u32[]{:S(2)}) collective-permute-start(bf16[4,128,128]{2,1,0:T(8,128)(2,1)S(1)} %copy.100), channel_id=1, source_target_pairs={{0,16},{4,20},{8,24},{12,28},{16,32},{20,36},{24,40},{28,44},{32,4... | collective-permute-start | bytes 393224 | tf_op jit(solution)/shard_map/while/body/eval_jaxpr/ppermute | solution.py:14
  112.3 18.3 %collective-permute-start.2 = (f32[4,128,128]{2,1,0:T(8,128)S(1)}, f32[4,128,128]{2,1,0:T(8,128)S(1)}, u32[]{:S(2)}, u32[]{:S(2)}) collective-permute-start(f32[4,128,128]{2,1,0:T(8,128)S(1)} %maximum_add_fusion.6), channel_id=1, source_target_pairs={{0,16},{4,20},{8,24},{12,28},{16,32},{20,36},{24,40},{28,44},{32,4... | collective-permute-start | bytes 786440 | tf_op jit(solution)/shard_map/while/body/eval_jaxpr/ppermute | solution.py:14
  114.9 18.5 %collective-permute-start.3 = (f32[4,128,128]{2,1,0:T(8,128)}, f32[4,128,128]{2,1,0:T(8,128)S(1)}, u32[]{:S(2)}, u32[]{:S(2)}) collective-permute-start(f32[4,128,128]{2,1,0:T(8,128)} %maximum_add_fusion.7), channel_id=1, source_target_pairs={{0,16},{4,20},{8,24},{12,28},{16,32},{20,36},{24,40},{28,44},{32,4... | collective-permute-start | bytes 786440 | tf_op jit(solution)/shard_map/while/body/eval_jaxpr/ppermute | solution.py:14
  135.1 15.7 %collective-permute-start = (bf16[4,128,128]{2,1,0:T(8,128)(2,1)S(1)}, bf16[4,128,128]{2,1,0:T(8,128)(2,1)}, u32[]{:S(2)}, u32[]{:S(2)}) collective-permute-start(bf16[4,128,128]{2,1,0:T(8,128)(2,1)S(1)} %copy.99), channel_id=1, source_target_pairs={{0,16},{4,20},{8,24},{12,28},{16,32},{20,36},{24,40},{28,44},{32,4... | collective-permute-start | bytes 393224 | tf_op jit(solution)/shard_map/while/body/eval_jaxpr/ppermute | solution.py:14
  137.9 16.5 %collective-permute-start.1 = (bf16[4,128,128]{2,1,0:T(8,128)(2,1)S(1)}, bf16[4,128,128]{2,1,0:T(8,128)(2,1)}, u32[]{:S(2)}, u32[]{:S(2)}) collective-permute-start(bf16[4,128,128]{2,1,0:T(8,128)(2,1)S(1)} %copy.100), channel_id=1, source_target_pairs={{0,16},{4,20},{8,24},{12,28},{16,32},{20,36},{24,40},{28,44},{32,4... | collective-permute-start | bytes 393224 | tf_op jit(solution)/shard_map/while/body/eval_jaxpr/ppermute | solution.py:14
  143.6 18.3 %collective-permute-start.2 = (f32[4,128,128]{2,1,0:T(8,128)S(1)}, f32[4,128,128]{2,1,0:T(8,128)S(1)}, u32[]{:S(2)}, u32[]{:S(2)}) collective-permute-start(f32[4,128,128]{2,1,0:T(8,128)S(1)} %maximum_add_fusion.6), channel_id=1, source_target_pairs={{0,16},{4,20},{8,24},{12,28},{16,32},{20,36},{24,40},{28,44},{32,4... | collective-permute-start | bytes 786440 | tf_op jit(solution)/shard_map/while/body/eval_jaxpr/ppermute | solution.py:14
  146.2 18.5 %collective-permute-start.3 = (f32[4,128,128]{2,1,0:T(8,128)}, f32[4,128,128]{2,1,0:T(8,128)S(1)}, u32[]{:S(2)}, u32[]{:S(2)}) collective-permute-start(f32[4,128,128]{2,1,0:T(8,128)} %maximum_add_fusion.7), channel_id=1, source_target_pairs={{0,16},{4,20},{8,24},{12,28},{16,32},{20,36},{24,40},{28,44},{32,4... | collective-permute-start | bytes 786440 | tf_op jit(solution)/shard_map/while/body/eval_jaxpr/ppermute | solution.py:14
  169.2 16.5 %collective-permute-start.1 = (bf16[4,128,128]{2,1,0:T(8,128)(2,1)S(1)}, bf16[4,128,128]{2,1,0:T(8,128)(2,1)}, u32[]{:S(2)}, u32[]{:S(2)}) collective-permute-start(bf16[4,128,128]{2,1,0:T(8,128)(2,1)S(1)} %copy.100), channel_id=1, source_target_pairs={{0,16},{4,20},{8,24},{12,28},{16,32},{20,36},{24,40},{28,44},{32,4... | collective-permute-start | bytes 393224 | tf_op jit(solution)/shard_map/while/body/eval_jaxpr/ppermute | solution.py:14
  174.9 18.3 %collective-permute-start.2 = (f32[4,128,128]{2,1,0:T(8,128)S(1)}, f32[4,128,128]{2,1,0:T(8,128)S(1)}, u32[]{:S(2)}, u32[]{:S(2)}) collective-permute-start(f32[4,128,128]{2,1,0:T(8,128)S(1)} %maximum_add_fusion.6), channel_id=1, source_target_pairs={{0,16},{4,20},{8,24},{12,28},{16,32},{20,36},{24,40},{28,44},{32,4... | collective-permute-start | bytes 786440 | tf_op jit(solution)/shard_map/while/body/eval_jaxpr/ppermute | solution.py:14
  177.5 18.5 %collective-permute-start.3 = (f32[4,128,128]{2,1,0:T(8,128)}, f32[4,128,128]{2,1,0:T(8,128)S(1)}, u32[]{:S(2)}, u32[]{:S(2)}) collective-permute-start(f32[4,128,128]{2,1,0:T(8,128)} %maximum_add_fusion.7), channel_id=1, source_target_pairs={{0,16},{4,20},{8,24},{12,28},{16,32},{20,36},{24,40},{28,44},{32,4... | collective-permute-start | bytes 786440 | tf_op jit(solution)/shard_map/while/body/eval_jaxpr/ppermute | solution.py:14
  200.5 16.5 %collective-permute-start.1 = (bf16[4,128,128]{2,1,0:T(8,128)(2,1)S(1)}, bf16[4,128,128]{2,1,0:T(8,128)(2,1)}, u32[]{:S(2)}, u32[]{:S(2)}) collective-permute-start(bf16[4,128,128]{2,1,0:T(8,128)(2,1)S(1)} %copy.100), channel_id=1, source_target_pairs={{0,16},{4,20},{8,24},{12,28},{16,32},{20,36},{24,40},{28,44},{32,4... | collective-permute-start | bytes 393224 | tf_op jit(solution)/shard_map/while/body/eval_jaxpr/ppermute | solution.py:14
  206.2 18.3 %collective-permute-start.2 = (f32[4,128,128]{2,1,0:T(8,128)S(1)}, f32[4,128,128]{2,1,0:T(8,128)S(1)}, u32[]{:S(2)}, u32[]{:S(2)}) collective-permute-start(f32[4,128,128]{2,1,0:T(8,128)S(1)} %maximum_add_fusion.6), channel_id=1, source_target_pairs={{0,16},{4,20},{8,24},{12,28},{16,32},{20,36},{24,40},{28,44},{32,4... | collective-permute-start | bytes 786440 | tf_op jit(solution)/shard_map/while/body/eval_jaxpr/ppermute | solution.py:14
  208.8 18.5 %collective-permute-start.3 = (f32[4,128,128]{2,1,0:T(8,128)}, f32[4,128,128]{2,1,0:T(8,128)S(1)}, u32[]{:S(2)}, u32[]{:S(2)}) collective-permute-start(f32[4,128,128]{2,1,0:T(8,128)} %maximum_add_fusion.7), channel_id=1, source_target_pairs={{0,16},{4,20},{8,24},{12,28},{16,32},{20,36},{24,40},{28,44},{32,4... | collective-permute-start | bytes 786440 | tf_op jit(solution)/shard_map/while/body/eval_jaxpr/ppermute | solution.py:14
  231.8 16.5 %collective-permute-start.1 = (bf16[4,128,128]{2,1,0:T(8,128)(2,1)S(1)}, bf16[4,128,128]{2,1,0:T(8,128)(2,1)}, u32[]{:S(2)}, u32[]{:S(2)}) collective-permute-start(bf16[4,128,128]{2,1,0:T(8,128)(2,1)S(1)} %copy.100), channel_id=1, source_target_pairs={{0,16},{4,20},{8,24},{12,28},{16,32},{20,36},{24,40},{28,44},{32,4... | collective-permute-start | bytes 393224 | tf_op jit(solution)/shard_map/while/body/eval_jaxpr/ppermute | solution.py:14
  237.5 18.3 %collective-permute-start.2 = (f32[4,128,128]{2,1,0:T(8,128)S(1)}, f32[4,128,128]{2,1,0:T(8,128)S(1)}, u32[]{:S(2)}, u32[]{:S(2)}) collective-permute-start(f32[4,128,128]{2,1,0:T(8,128)S(1)} %maximum_add_fusion.6), channel_id=1, source_target_pairs={{0,16},{4,20},{8,24},{12,28},{16,32},{20,36},{24,40},{28,44},{32,4... | collective-permute-start | bytes 786440 | tf_op jit(solution)/shard_map/while/body/eval_jaxpr/ppermute | solution.py:14
  240.1 18.5 %collective-permute-start.3 = (f32[4,128,128]{2,1,0:T(8,128)}, f32[4,128,128]{2,1,0:T(8,128)S(1)}, u32[]{:S(2)}, u32[]{:S(2)}) collective-permute-start(f32[4,128,128]{2,1,0:T(8,128)} %maximum_add_fusion.7), channel_id=1, source_target_pairs={{0,16},{4,20},{8,24},{12,28},{16,32},{20,36},{24,40},{28,44},{32,4... | collective-permute-start | bytes 786440 | tf_op jit(solution)/shard_map/while/body/eval_jaxpr/ppermute | solution.py:14
  263.1 16.5 %collective-permute-start.1 = (bf16[4,128,128]{2,1,0:T(8,128)(2,1)S(1)}, bf16[4,128,128]{2,1,0:T(8,128)(2,1)}, u32[]{:S(2)}, u32[]{:S(2)}) collective-permute-start(bf16[4,128,128]{2,1,0:T(8,128)(2,1)S(1)} %copy.100), channel_id=1, source_target_pairs={{0,16},{4,20},{8,24},{12,28},{16,32},{20,36},{24,40},{28,44},{32,4... | collective-permute-start | bytes 393224 | tf_op jit(solution)/shard_map/while/body/eval_jaxpr/ppermute | solution.py:14
  268.8 18.3 %collective-permute-start.2 = (f32[4,128,128]{2,1,0:T(8,128)S(1)}, f32[4,128,128]{2,1,0:T(8,128)S(1)}, u32[]{:S(2)}, u32[]{:S(2)}) collective-permute-start(f32[4,128,128]{2,1,0:T(8,128)S(1)} %maximum_add_fusion.6), channel_id=1, source_target_pairs={{0,16},{4,20},{8,24},{12,28},{16,32},{20,36},{24,40},{28,44},{32,4... | collective-permute-start | bytes 786440 | tf_op jit(solution)/shard_map/while/body/eval_jaxpr/ppermute | solution.py:14
  271.4 18.5 %collective-permute-start.3 = (f32[4,128,128]{2,1,0:T(8,128)}, f32[4,128,128]{2,1,0:T(8,128)S(1)}, u32[]{:S(2)}, u32[]{:S(2)}) collective-permute-start(f32[4,128,128]{2,1,0:T(8,128)} %maximum_add_fusion.7), channel_id=1, source_target_pairs={{0,16},{4,20},{8,24},{12,28},{16,32},{20,36},{24,40},{28,44},{32,4... | collective-permute-start | bytes 786440 | tf_op jit(solution)/shard_map/while/body/eval_jaxpr/ppermute | solution.py:14
  294.4 16.6 %collective-permute-start.1 = (bf16[4,128,128]{2,1,0:T(8,128)(2,1)S(1)}, bf16[4,128,128]{2,1,0:T(8,128)(2,1)}, u32[]{:S(2)}, u32[]{:S(2)}) collective-permute-start(bf16[4,128,128]{2,1,0:T(8,128)(2,1)S(1)} %copy.100), channel_id=1, source_target_pairs={{0,16},{4,20},{8,24},{12,28},{16,32},{20,36},{24,40},{28,44},{32,4... | collective-permute-start | bytes 393224 | tf_op jit(solution)/shard_map/while/body/eval_jaxpr/ppermute | solution.py:14
  300.1 18.4 %collective-permute-start.2 = (f32[4,128,128]{2,1,0:T(8,128)S(1)}, f32[4,128,128]{2,1,0:T(8,128)S(1)}, u32[]{:S(2)}, u32[]{:S(2)}) collective-permute-start(f32[4,128,128]{2,1,0:T(8,128)S(1)} %maximum_add_fusion.6), channel_id=1, source_target_pairs={{0,16},{4,20},{8,24},{12,28},{16,32},{20,36},{24,40},{28,44},{32,4... | collective-permute-start | bytes 786440 | tf_op jit(solution)/shard_map/while/body/eval_jaxpr/ppermute | solution.py:14
  302.7 18.6 %collective-permute-start.3 = (f32[4,128,128]{2,1,0:T(8,128)}, f32[4,128,128]{2,1,0:T(8,128)S(1)}, u32[]{:S(2)}, u32[]{:S(2)}) collective-permute-start(f32[4,128,128]{2,1,0:T(8,128)} %maximum_add_fusion.7), channel_id=1, source_target_pairs={{0,16},{4,20},{8,24},{12,28},{16,32},{20,36},{24,40},{28,44},{32,4... | collective-permute-start | bytes 786440 | tf_op jit(solution)/shard_map/while/body/eval_jaxpr/ppermute | solution.py:14
  324.2 21.3 %collective-permute-start.16 = (f32[2,128,128]{2,1,0:T(8,128)S(1)}, f32[2,128,128]{2,1,0:T(8,128)S(1)}, u32[]{:S(2)}, u32[]{:S(2)}) collective-permute-start(f32[2,128,128]{2,1,0:T(8,128)S(1)} %slice.236), channel_id=1, source_target_pairs={{0,504},{4,508},{8,0},{12,4},{16,8},{20,12},{24,16},{28,20},{32,24... | collective-permute-start | bytes 393224 | tf_op jit(solution)/shard_map/ppermute | solution.py:14
  (131 other events, 958.3 us)
